TPU v7x, 32 devices: a whole 2x2x4 slice. The times are simulated.
32 devices in a mesh: dp: 4 (over y, x), expert: 4 (over z), tensor: 2 (over core).
Axes of the slice: x: 2, y: 2, z: 4, core: 2. Of those that a mesh axis runs over, the one named last changes fastest.
Arguments:
- tokens: bfloat16 [2048, 7168], P(('dp', 'expert'), 'tensor'), may hold values from -6 to 6
- routing: int32 [2048, 2], P(('dp', 'expert')), may hold values from 0 to 3, all different within a row; in each aligned block of 128 rows (0 to 127, 128 to 255, ...) at most 72 rows name the same one
- gate_values: float32 [2048, 2], P(('dp', 'expert')), may hold values from 0.1 to 1
- expert_weight: bfloat16 [4, 7168, 1024], P('expert', 'tensor'), may hold values from -0.0625 to 0.0625
- subspace: bfloat16 [4, 64, 7168], P('expert', None, 'tensor'), may hold values from -0.0625 to 0.0625
- gradient: float32 [4, 2, 3584, 1024], P('expert', 'tensor', 'dp'), may hold values from -6 to 6
Outputs:
- combined: bfloat16 [2048, 1024], P(('dp', 'expert'), 'tensor')
- new_basis: float32 [4, 2, 64, 3584], P('expert', 'tensor', None, 'dp')
- preconditioned: float32 [4, 2, 3584, 1024], P('expert', 'tensor', 'dp')
Inputs may be any that keep to these rules, and one draw needn't show every extreme that they name: `routing`: each row names 2 different experts; in each device's aligned block of 128 rows no expert is named more than 72 times, a bound that some block reaches.
All inputs are finite; a program needn't handle non-finite values.
Results may differ from a plain program's by a relative error of at most 0.0049.
Values may be sent and summed in bfloat16 or wider, within the bound.
A program may use at most 64 MiB of HBM per device.

v0:
```python
import jax
import jax.numpy as jnp
from jax import lax
from jax.sharding import PartitionSpec as P

EPSILON = 1e-05


def tri_solve(factor, rhs, flip):
    return lax.linalg.triangular_solve(factor, rhs, left_side=True, lower=True, transpose_a=flip)


def finish(image_mine, diagonal, grad_rows, gram_matrix, curvature, inner_term, token_mean):
    highest = lax.Precision.HIGHEST
    factor_low = jnp.linalg.cholesky(gram_matrix)
    eigen_scale = jnp.diagonal(factor_low) / token_mean
    middle = jnp.dot(factor_low / eigen_scale[None, :], factor_low.T, precision=highest) + curvature
    factor_mid = jnp.linalg.cholesky(middle)
    solved = tri_solve(factor_mid, tri_solve(factor_mid, inner_term, False), True)
    scaled = image_mine / diagonal[None, :]
    result = grad_rows / diagonal[:, None] - jnp.dot(scaled.T, solved, precision=highest)
    basis_out = tri_solve(factor_low, image_mine, False)
    return (basis_out, result)


def body(tokens, routing, gate_values, expert_weight, subspace, gradient):
    highest = lax.Precision.HIGHEST
    tok_rows, half_width = tokens.shape
    choose_count = routing.shape[1]
    owners = lax.axis_size("expert")
    tensor_count = lax.axis_size("tensor")
    capacity = tok_rows * choose_count // owners * 9 // 8
    pair_count = tok_rows * choose_count
    slot_count = owners * capacity
    hidden_units = expert_weight.shape[2]
    flat_ids = routing.reshape(pair_count)
    one_hot = (flat_ids[:, None] == jnp.arange(owners, dtype=jnp.int32)[None, :]).astype(
        jnp.float32
    )
    pair_index = jnp.arange(pair_count, dtype=jnp.int32)
    strict_lower = (pair_index[:, None] > pair_index[None, :]).astype(jnp.float32)
    before = jnp.dot(strict_lower, one_hot, preferred_element_type=jnp.float32)
    position = jnp.sum(before * one_hot, axis=1).astype(jnp.int32)
    slot_ids = flat_ids * capacity + position
    matches = (jnp.arange(slot_count, dtype=jnp.int32)[:, None] == slot_ids[None, :]).reshape(
        slot_count, tok_rows, choose_count
    )
    picker = jnp.sum(matches.astype(jnp.float32), axis=2).astype(jnp.bfloat16)
    outgoing = jnp.dot(picker, tokens, preferred_element_type=jnp.float32).astype(jnp.bfloat16)
    outgoing = outgoing.reshape(owners, capacity, half_width)
    incoming = lax.all_to_all(outgoing, "expert", split_axis=0, concat_axis=0, tiled=True)
    slab_rows = incoming.reshape(slot_count, half_width)
    partial_value = jnp.dot(slab_rows, expert_weight[0], preferred_element_type=jnp.float32).astype(
        jnp.bfloat16
    )
    shaped = partial_value.reshape(owners, capacity, tensor_count, hidden_units // tensor_count)
    returned = lax.all_to_all(
        lax.all_to_all(shaped, "expert", split_axis=0, concat_axis=0, tiled=True),
        "tensor",
        split_axis=2,
        concat_axis=2,
        tiled=True,
    )
    hidden = jnp.sum(returned.astype(jnp.float32), axis=2).reshape(
        slot_count, hidden_units // tensor_count
    )
    weighting = jnp.sum(matches.astype(jnp.float32) * gate_values[None, :, :], axis=2).T
    combined = jnp.dot(weighting, hidden, precision=highest).astype(jnp.bfloat16)
    projected = lax.dot_general(
        slab_rows, subspace[0], (((1,), (1,)), ((), ())), preferred_element_type=jnp.float32
    ).astype(jnp.bfloat16)
    image_rows = lax.dot_general(
        projected, slab_rows, (((0,), (0,)), ((), ())), preferred_element_type=jnp.float32
    )
    square_sums = jnp.sum(jnp.square(slab_rows.astype(jnp.float32)), axis=0)
    stacked = jnp.concatenate([image_rows, square_sums[None, :]], axis=0)
    rank_rows = image_rows.shape[0]
    token_mean = float(tok_rows * choose_count * lax.axis_size("dp"))
    grad_rows = gradient[0, 0]
    summed = lax.psum_scatter(stacked, "dp", scatter_dimension=1, tiled=True)
    image_mine = summed[:rank_rows]
    diagonal = summed[rank_rows] / token_mean + EPSILON
    scaled = image_mine / diagonal[None, :]
    gram_part = jnp.dot(image_mine, image_mine.T, precision=highest)
    curve_part = jnp.dot(scaled, image_mine.T, precision=highest)
    inner_part = jnp.dot(scaled, grad_rows, precision=highest)
    gram_matrix, curvature, inner_term = lax.psum((gram_part, curve_part, inner_part), "dp")
    basis_out, result = finish(
        image_mine, diagonal, grad_rows, gram_matrix, curvature, inner_term, token_mean
    )
    return (combined, basis_out[None, None], result[None, None])


def solution(mesh):
    in_specs = (
        P(("dp", "expert"), "tensor"),
        P(("dp", "expert"), None),
        P(("dp", "expert"), None),
        P("expert", "tensor", None),
        P("expert", None, "tensor"),
        P("expert", "tensor", "dp", None),
    )
    out_specs = (
        P(("dp", "expert"), "tensor"),
        P("expert", "tensor", None, "dp"),
        P("expert", "tensor", "dp", None),
    )
    return jax.shard_map(body, mesh=mesh, in_specs=in_specs, out_specs=out_specs, check_vma=False)
```

profile of v0, /device:TPU:0, one launch (start us, length us, event | category | flops | bytes accessed | tf_op | source)
XLA Modules:
  0.0 205.4 jit_solution(8244849164581756324)
XLA Ops:
  7.2 0.0 copy-start
  7.2 0.0 reduce-scatter.2.cloned.1.call-start
  7.2 0.9 copy.57
  8.1 0.1 eq.30
  8.2 0.2 fusion.10
  8.4 0.1 convert_element_type.39
  8.6 0.1 copy.58
  8.6 0.7 multiply_add_fusion
  9.3 0.8 convert_reduce_fusion.1
  10.1 0.0 copy-done
  10.1 0.7 convolution_convert_fusion
  10.8 53.6 %all_to_all.15 = bf16[4,72,3584]{2,1,0:T(8,128)(2,1)S(1)} all-to-all(bf16[4,72,3584]{2,1,0:T(8,128)(2,1)S(1)} %bitcast.59), channel_id=1, replica_groups=mesh['dp'=4,'expert'=4,'tensor'=2] {'expert'}, dimensions={0} | all-to-all | bytes 4128768 | tf_op jit(solution)/shard_map/all_to_all | solution.py:51
  64.4 0.4 multiply_reduce_fusion
  64.9 3.9 %fusion.9 = f32[64,3584]{1,0:T(8,128)} fusion(bf16[288,3584]{1,0:T(8,128)(2,1)S(1)} %bitcast.57, bf16[1,64,3584]{2,1,0:T(8,128)(2,1)} %param.11), kind=kOutput, calls=%fused_computation.15 | convolution fusion | flops 264259584 | bytes 3440640 | tf_op jit(solution)/shard_map/dot_general | solution.py:72
  68.8 2.2 %pad_maximum_fusion = f32[65,3584]{1,0:T(8,128)} fusion(f32[1,3584]{1,0:T(1,128)S(1)} %broadcast_in_dim.8, f32[64,3584]{1,0:T(8,128)} %fusion.9), kind=kLoop, calls=%fused_computation.19 | loop fusion | flops 232960 | bytes 1863680 | tf_op jit(solution)/shard_map/concatenate | solution.py:76
  71.0 0.0 reduce-scatter.2.cloned.1.call-update
  71.0 6.2 %fusion.6 = bf16[288,1024]{1,0:T(8,128)(2,1)} fusion(bf16[288,3584]{1,0:T(8,128)(2,1)S(1)} %bitcast.58, bf16[1,3584,1024]{2,1,0:T(8,128)(2,1)} %param.10), kind=kOutput, calls=%fused_computation.10 | convolution fusion | flops 2114224128 | bytes 9994240 | tf_op jit(solution)/shard_map/dot_general | solution.py:53
  77.2 2.2 %reshape.68 = bf16[4,72,2,512]{3,2,1,0:T(2,128)(2,1)S(1)} reshape(bf16[288,1024]{1,0:T(8,128)(2,1)} %fusion.6) | data formatting | bytes 1179648 | tf_op jit(solution)/shard_map/reshape | solution.py:56
  79.4 0.9 copy.59
  80.3 3.5 %all-to-all-start.1 = ((bf16[4,72,2,512]{3,1,2,0:T(8,128)(2,1)}), bf16[4,72,2,512]{3,1,2,0:T(8,128)(2,1)S(1)}, u32[]{:S(2)}, u32[]{:S(2)}) async-start(bf16[4,72,2,512]{3,1,2,0:T(8,128)(2,1)} %copy.59), calls=%async_computation.1 | async-start | bytes 1179648 | tf_op jit(solution)/shard_map/all_to_all | solution.py:58
  83.8 0.0 all-reduce.3.cloned.1.call-start
  83.8 15.0 %all-to-all-done.1 = bf16[4,72,2,512]{3,1,2,0:T(8,128)(2,1)S(1)} async-done(((bf16[4,72,2,512]{3,1,2,0:T(8,128)(2,1)}), bf16[4,72,2,512]{3,1,2,0:T(8,128)(2,1)S(1)}, u32[]{:S(2)}, u32[]{:S(2)}) %all-to-all-start.1) | async-done | bytes 589856 | tf_op jit(solution)/shard_map/all_to_all | solution.py:58
  98.9 4.2 %all_to_all.16 = bf16[4,72,2,512]{3,1,0,2:T(8,128)(2,1)S(1)} all-to-all(bf16[4,72,2,512]{3,1,0,2:T(8,128)(2,1)S(1)} %copy.60), channel_id=1, replica_groups=mesh['dp'=4,'expert'=4,'tensor'=2] {'tensor'}, dimensions={2} | all-to-all | bytes 1179648 | tf_op jit(solution)/shard_map/all_to_all | solution.py:57
  103.1 0.1 convert_reduce_fusion
  103.2 1.3 convolution_convert_fusion.1
  104.5 0.0 reduce-scatter.2.cloned.1.call-done
  104.5 0.0 copy-start.1
  104.5 0.8 fusion.30
  105.3 1.4 fusion.16
  106.7 1.4 fusion.13
  108.2 17.0 %all-reduce = (f32[64,64]{0,1:T(8,128)S(1)}, f32[64,64]{0,1:T(8,128)S(1)}) all-reduce(f32[64,64]{0,1:T(8,128)S(1)} %fusion.16, f32[64,64]{0,1:T(8,128)S(1)} %fusion.13), channel_id=1, replica_groups=mesh['dp'=4,'expert'=4,'tensor'=2] {'dp'}, use_global_device_ids=true, to_apply=%region_6.0 | all-reduce | flops 8192 | bytes 65536 | tf_op jit(solution)/shard_map/psum | solution.py:87
  125.1 0.1 copy.62
  125.2 5.8 %cholesky.44 = f32[64,64]{1,0:T(8,128)S(1)} custom-call(f32[64,64]{1,0:T(8,128)S(1)} %fusion.27), custom_call_target="Cholesky" | custom-call | tf_op jit(solution)/shard_map/jit(cholesky)/cholesky | solution.py:15
  131.1 0.6 compare_reduce_fusion.1
  131.8 0.7 select_bitcast_fusion
  132.4 4.9 %custom-call.10 = f32[1,64,64]{1,2,0:T(8,128)S(1)} custom-call(f32[1,64,64]{2,1,0:T(8,128)S(1)} %get-tuple-element.8), custom_call_target="InvertDiagBlocksLowerTriangular" | custom-call | tf_op jit(solution)/shard_map/triangular_solve | solution.py:10
  137.3 0.8 gather_fusion
  138.1 0.2 convolution_add_fusion
  138.3 0.1 copy.65
  138.4 5.8 %cholesky.55 = f32[64,64]{1,0:T(8,128)S(1)} custom-call(f32[64,64]{1,0:T(8,128)S(1)} %fusion.25), custom_call_target="Cholesky" | custom-call | tf_op jit(solution)/shard_map/jit(cholesky)/cholesky | solution.py:18
  144.3 0.6 compare_reduce_fusion
  145.0 5.2 %fusion.2 = f32[64,1024]{1,0:T(8,128)} fusion(f32[1,1,896,1024]{3,2,1,0:T(8,128)} %param.12, f32[65,896]{1,0:T(8,128)} %reduce-scatter.2.cloned.1.call-done, f32[896]{0:T(1024)S(1)} %fusion.30), kind=kOutput, calls=%fused_computation.5 | convolution fusion | flops 704700416 | bytes 4165120 | tf_op jit(solution)/shard_map/dot_general | solution.py:86
  150.2 0.0 all-reduce.3.cloned.1.call-update
  150.2 0.7 fusion.20
  150.9 4.9 %custom-call.11 = f32[1,64,64]{1,2,0:T(8,128)S(1)} custom-call(f32[1,64,64]{2,1,0:T(8,128)S(1)} %fusion.20), custom_call_target="InvertDiagBlocksLowerTriangular" | custom-call | tf_op jit(solution)/shard_map/triangular_solve | solution.py:10
  155.8 0.0 copy-done.1
  155.8 1.1 convolution_bitcast_fusion
  156.9 33.8 %all-reduce.3.cloned.1.call-done = f32[64,1024]{1,0:T(8,128)} async-done(((f32[64,1024]{1,0:T(8,128)}), f32[64,1024]{1,0:T(8,128)}) %all-reduce.3.cloned.1.call-update) | async-done | bytes 262160 | tf_op jit(solution)/shard_map/psum | solution.py:87
  190.7 1.4 fusion.23
  192.1 0.4 fusion.21
  192.4 6.2 %fusion.5 = f32[1,1,896,1024]{3,2,1,0:T(8,128)} fusion(f32[1,1,896,1024]{3,2,1,0:T(8,128)} %param.12, f32[64,1024]{1,0:T(8,128)S(1)} %fusion.21, f32[896]{0:T(1024)S(1)} %fusion.30, f32[65,896]{1,0:T(8,128)S(1)} %copy-done.1), kind=kOutput, calls=%fused_computation.9 | convolution fusion | flops 706535424 | bytes 7839744 | tf_op jit(solution)/shard_map/dot_general | solution.py:21
  (9 shorter events, 0.2 us)
Async XLA Ops:
  7.2 2.9 %copy-start = (bf16[128,3584]{1,0:T(8,128)(2,1)S(1)}, bf16[128,3584]{1,0:T(8,128)(2,1)}, u32[]{:S(2)}) copy-start(bf16[128,3584]{1,0:T(8,128)(2,1)} %param.7) | copy-start | bytes 2752516
  7.2 97.3 %reduce-scatter.2.cloned.1.call-start = ((), (), s32[]{:S(2)}) async-start(), calls=%async_computation.4 | async-start | bytes 1290240 | tf_op jit(solution)/shard_map/reduce_scatter | solution.py:80
  80.3 18.6 %all-to-all-start.1 = ((bf16[4,72,2,512]{3,1,2,0:T(8,128)(2,1)}), bf16[4,72,2,512]{3,1,2,0:T(8,128)(2,1)S(1)}, u32[]{:S(2)}, u32[]{:S(2)}) async-start(bf16[4,72,2,512]{3,1,2,0:T(8,128)(2,1)} %copy.59), calls=%async_computation.1 | async-start | bytes 1179648 | tf_op jit(solution)/shard_map/all_to_all | solution.py:58
  83.8 106.9 %all-reduce.3.cloned.1.call-start = ((), (), s32[]{:S(2)}) async-start(), calls=%async_computation.5 | async-start | bytes 524288 | tf_op jit(solution)/shard_map/psum | solution.py:87
  104.5 51.3 %copy-start.1 = (f32[65,896]{1,0:T(8,128)S(1)}, f32[65,896]{1,0:T(8,128)}, u32[]{:S(2)}) copy-start(f32[65,896]{1,0:T(8,128)} %reduce-scatter.2.cloned.1.call-done) | copy-start | bytes 698884
Sparse Core Ops, SparseCore 0:
  71.1 26.9 reduce-scatter.1
  150.3 40.3 all-reduce.2
where the time goes:
time: 206 us; the launch traced here: 205 us
  blocking collectives  74.8 us (36%)
  waiting for transfers between devices  48.9 us (24%)
  matrix products  29.4 us (14%)
  other arithmetic  29.2 us (14%)
  between operations  14.2 us (7%)
  local copies, waits for them, and re-layouts  5.3 us (3%)
  starting transfers between devices  3.56 us (2%)
    all_to_all x1, blocking collectives, body(): lax.all_to_all(outgoing, 'expert', split_axis=0, concat_axis=0, tiled=True)  53.6 us
    psum x1, waiting for transfers between devices, body(): lax.psum((gram_part, curve_part, inner_part), 'dp')  33.8 us
    psum x1, blocking collectives, body(): lax.psum((gram_part, curve_part, inner_part), 'dp')  17 us
    all_to_all x1, waiting for transfers between devices, body(): lax.all_to_all(shaped, 'expert', split_axis=0, concat_axis=0, tiled=True)  15 us
    another operation x4, other arithmetic, tri_solve(): lax.linalg.triangular_solve(factor, rhs, left_side=True, lower=True, tran...  11.1 us
    another operation x3, other arithmetic, finish(): factor_low = jnp.linalg.cholesky(gram_matrix)  6.52 us
    another operation x3, other arithmetic, finish(): factor_mid = jnp.linalg.cholesky(middle)  6.52 us
    dot_general x1, matrix products, body(): jnp.dot(slab_rows, expert_weight[0], preferred_element_type=jnp.float32)  6.19 us
  transfers between devices with their start and end apart: 3, of which 2 were waited for; matrix products, arithmetic and copies ran while one was open for 8% of the time, Pallas kernels for 0%

commit v1 on v0

--- a/solution.py
+++ b/solution.py
@@ -1,6 +1,10 @@
+import functools
+
 import jax
 import jax.numpy as jnp
 from jax import lax
+from jax.experimental import pallas as pl
+from jax.experimental.pallas import tpu as pltpu
 from jax.sharding import PartitionSpec as P
 
 EPSILON = 1e-05
@@ -91,6 +95,315 @@
     return (combined, basis_out[None, None], result[None, None])
 
 
+HIGHEST = lax.Precision.HIGHEST
+MESH = pl.DeviceIdType.MESH
+
+
+def is_power(n):
+    return n & (n - 1) == 0
+
+
+def fits(sizes, tokens, subspace, gradient, expert_weight):
+    few = sizes["dp"] <= 4 and sizes["expert"] <= 4 and sizes["tensor"] == 2
+    even = is_power(sizes["dp"]) and is_power(sizes["expert"])
+    lanes = gradient.shape[2] % 128 == 0 and expert_weight.shape[2] % 256 == 0
+    return few and even and lanes and subspace.shape[1] == 64 and tokens.shape[0] == 128
+
+
+def flip(index, k, n):
+    out, bit = 0, 1
+    while bit < n:
+        own = lax.rem(index // bit, 2)
+        out = out + bit * (1 - own if (k // bit) % 2 else own)
+        bit *= 2
+    return out
+
+
+def split(x):
+    high = x.astype(jnp.bfloat16)
+    low = (x - high.astype(jnp.float32)).astype(jnp.bfloat16)
+    return high, low
+
+
+def f32_dot(a, b, dims):
+    return lax.dot_general(a, b, (dims, ((), ())), preferred_element_type=jnp.float32)
+
+
+def eliminate(matrix, work):
+    rank = matrix.shape[0]
+    row_id = lax.broadcasted_iota(jnp.int32, (rank, 2 * rank), 0)
+    lane_id = lax.broadcasted_iota(jnp.int32, (rank, 2 * rank), 1)
+    eye = (lax.broadcasted_iota(jnp.int32, (rank, rank), 0) == lax.broadcasted_iota(jnp.int32, (rank, rank), 1)).astype(jnp.float32)
+    work[...] = jnp.concatenate([matrix, eye], axis=1)
+
+    def step(j, state):
+        row = work[pl.ds(j, 1), :]
+        pivot = jnp.sum(jnp.where(lane_id[:1] == j, row, 0.0), axis=1, keepdims=True)
+        column = jnp.sum(jnp.where(lane_id == j, state, 0.0), axis=1, keepdims=True)
+        factor = jnp.where(row_id[:, :1] > j, column, 0.0) / pivot
+        state = state - factor * row
+        work[...] = state
+        return state
+
+    state = lax.fori_loop(0, rank, step, work[...])
+    return state[:, :rank], state[:, rank:], jnp.sum(state[:, :rank] * eye, axis=1, keepdims=True)
+
+
+def exchange(n_dp, n_exp, cap, token_mean, tok_hbm, route_ref, gate_ref, w_hbm, sub_hbm, grad_hbm,
+             comb_ref, basis_ref, solved_ref, scaled_ref, recip_ref,
+             tok, sub, wgt, grad, g_high, g_low, out_rows, in_rows, parts, ret, image, rs_in, small, small_in,
+             inner, inner_in, work, loc_sem, tok_s, tok_r, ret_s, ret_r, rs_s, rs_r, sm_s, sm_r, in_s, in_r):
+    dp = lax.axis_index("dp")
+    ex = lax.axis_index("expert")
+    core = lax.axis_index("tensor")
+    half = parts.shape[3]
+    width = tok.shape[1]
+    chunk = width // n_dp
+    rank = sub.shape[0]
+    rows = tok.shape[0]
+
+    loads = [
+        pltpu.make_async_copy(tok_hbm, tok, loc_sem.at[0]),
+        pltpu.make_async_copy(sub_hbm, sub, loc_sem.at[1]),
+        pltpu.make_async_copy(w_hbm, wgt, loc_sem.at[2]),
+        pltpu.make_async_copy(grad_hbm, grad, loc_sem.at[3]),
+    ]
+    for load in loads:
+        load.start()
+
+    barrier = pltpu.get_barrier_semaphore()
+    peers = [(dp, flip(ex, k, n_exp), core) for k in range(1, n_exp)]
+    peers += [(dp, flip(ex, k, n_exp), 1 - core) for k in range(n_exp)]
+    peers += [(flip(dp, k, n_dp), ex, core) for k in range(1, n_dp)]
+    for peer in peers:
+        pl.semaphore_signal(barrier, inc=1, device_id=peer, device_id_type=MESH)
+
+    row_i = lax.broadcasted_iota(jnp.int32, (rows, rows), 0)
+    col_i = lax.broadcasted_iota(jnp.int32, (rows, rows), 1)
+    earlier = (row_i < col_i).astype(jnp.float32)
+    slot_i = lax.broadcasted_iota(jnp.int32, (cap, rows), 0)
+    named = []
+    for k in range(n_exp):
+        hit = route_ref[...] == flip(ex, k, n_exp)
+        named.append(jnp.sum(hit.astype(jnp.float32), axis=0, keepdims=True))
+    named8 = jnp.concatenate(named + [jnp.zeros((8 - n_exp, rows), jnp.float32)], axis=0)
+    before = f32_dot(named8.astype(jnp.bfloat16), earlier.astype(jnp.bfloat16), ((1,), (0,)))
+
+    def picker(k):
+        place = before[k:k + 1].astype(jnp.int32)
+        return jnp.where((slot_i == place) & (named8[k:k + 1] > 0.5), 1.0, 0.0).astype(jnp.bfloat16)
+
+    pickers = [picker(k) for k in range(n_exp)]
+    loads[0].wait()
+    pl.semaphore_wait(barrier, len(peers))
+
+    sends = []
+
+    def send(src, dst, s, r, peer):
+        copy = pltpu.make_async_remote_copy(
+            src_ref=src, dst_ref=dst, send_sem=s, recv_sem=r, device_id=peer, device_id_type=MESH
+        )
+        copy.start()
+        return copy
+
+    tok_copies = {}
+    for k in list(range(n_exp - 1, 0, -1)):
+        out_rows[k - 1] = f32_dot(pickers[k], tok[...], ((1,), (0,))).astype(jnp.bfloat16)
+        tok_copies[k] = send(out_rows.at[k - 1], in_rows.at[k], tok_s.at[k], tok_r.at[k], (dp, flip(ex, k, n_exp), core))
+    in_rows[0] = f32_dot(pickers[0], tok[...], ((1,), (0,))).astype(jnp.bfloat16)
+    loads[1].wait()
+
+    def add_image(k):
+        got = in_rows.at[k]
+        projected = f32_dot(got[...], sub[...], ((1,), (1,))).astype(jnp.bfloat16)
+        for j in range(n_dp):
+            part = got[:, j * chunk:(j + 1) * chunk]
+            img = f32_dot(projected, part, ((0,), (0,)))
+            wide = part.astype(jnp.float32)
+            sq = jnp.sum(wide * wide, axis=0, keepdims=True)
+            if k == 0:
+                image[j, :rank] = img
+                image[j, rank:rank + 8] = jnp.broadcast_to(sq, (8, chunk))
+            else:
+                image[j, :rank] += img
+                image[j, rank:rank + 8] += jnp.broadcast_to(sq, (8, chunk))
+
+    ret_copies = {}
+
+    def project(k):
+        for rel in range(2):
+            which = core if rel == 0 else 1 - core
+            cols = pl.ds(pl.multiple_of(which * half, half), half)
+            value = f32_dot(in_rows[k], wgt[:, cols], ((1,), (0,))).astype(jnp.bfloat16)
+            if k == 0 and rel == 0:
+                ret[0, 0] = value
+            else:
+                parts[k, rel] = value
+                peer = (dp, flip(ex, k, n_exp), which)
+                ret_copies[k, rel] = send(parts.at[k, rel], ret.at[k, rel], ret_s.at[k, rel], ret_r.at[k, rel], peer)
+
+    add_image(0)
+    loads[2].wait()
+    project(0)
+    loads[3].wait()
+    high, low = split(grad[...])
+    g_high[...] = high
+    g_low[...] = low
+    order = list(range(1, n_exp))
+    for k in order:
+        tok_copies[k].wait_recv()
+        add_image(k)
+        if k != order[-1]:
+            project(k)
+
+    rs_copies = {}
+    for k in range(n_dp - 1, 0, -1):
+        to = flip(dp, k, n_dp)
+        rs_copies[k] = send(image.at[to], rs_in.at[k], rs_s.at[k], rs_r.at[k], (to, ex, core))
+    project(order[-1])
+    total = image[dp]
+    for k in range(1, n_dp):
+        rs_copies[k].wait_recv()
+        total = total + rs_in[k]
+    mine = total[:rank]
+    recip = 1.0 / (total[rank:rank + 1] / token_mean + EPSILON)
+    scaled = mine * recip
+    both = jnp.concatenate([mine, scaled], axis=0)
+    small[...] = lax.dot_general(mine, both, (((1,), (1,)), ((), ())), precision=HIGHEST, preferred_element_type=jnp.float32)
+    sm_copies = {}
+    for k in range(n_dp - 1, 0, -1):
+        sm_copies[k] = send(small, small_in.at[k], sm_s.at[k], sm_r.at[k], (flip(dp, k, n_dp), ex, core))
+    s_high, s_low = split(scaled)
+    s_both = jnp.concatenate([s_high, s_low], axis=0)
+    cross = f32_dot(s_both, g_high[...], ((1,), (0,)))
+    inner[...] = cross[:rank] + cross[rank:] + f32_dot(s_high, g_low[...], ((1,), (0,)))
+    in_copies = {}
+    for k in range(n_dp - 1, 0, -1):
+        in_copies[k] = send(inner, inner_in.at[k], in_s.at[k], in_r.at[k], (flip(dp, k, n_dp), ex, core))
+    scaled_ref[...] = scaled
+    recip_ref[...] = jnp.broadcast_to(recip, (8, chunk))
+
+    sums = small[...]
+    for k in range(1, n_dp):
+        sm_copies[k].wait_recv()
+        sums = sums + small_in[k]
+    upper, lower_inv, pivots = eliminate(sums[:, :rank], work)
+    root = lax.rsqrt(pivots)
+    transposed = upper * root
+    basis_ref[...] = root * lax.dot_general(lower_inv, mine, (((1,), (0,)), ((), ())), precision=HIGHEST, preferred_element_type=jnp.float32)
+    middle = lax.dot_general(transposed * (root * token_mean), transposed, (((0,), (0,)), ((), ())), precision=HIGHEST, preferred_element_type=jnp.float32)
+    middle = middle + sums[:, rank:]
+    _, mid_inv, mid_pivots = eliminate(middle, work)
+    inverse = lax.dot_general(mid_inv / mid_pivots, mid_inv, (((0,), (0,)), ((), ())), precision=HIGHEST, preferred_element_type=jnp.float32)
+
+    gates = []
+    for k in range(n_exp):
+        hit = (route_ref[...] == flip(ex, k, n_exp)).astype(jnp.float32)
+        gates.append(jnp.sum(hit * gate_ref[...], axis=0, keepdims=True))
+    gates8 = jnp.concatenate(gates + [jnp.zeros((8 - n_exp, rows), jnp.float32)], axis=0)
+    gate_cols = gates8.T
+    combined = jnp.zeros((rows, half), jnp.float32)
+    for k in range(n_exp):
+        hidden = jnp.zeros((rows, half), jnp.float32)
+        for rel in range(2):
+            if (k, rel) in ret_copies:
+                ret_copies[k, rel].wait_recv()
+            hidden = hidden + f32_dot(pickers[k], ret[k, rel], ((0,), (0,)))
+        combined = combined + gate_cols[:, k:k + 1] * hidden
+    comb_ref[...] = combined.astype(jnp.bfloat16)
+
+    inner_sum = inner[...]
+    for k in range(1, n_dp):
+        in_copies[k].wait_recv()
+        inner_sum = inner_sum + inner_in[k]
+    solved_ref[...] = lax.dot_general(inverse, inner_sum, (((1,), (0,)), ((), ())), precision=HIGHEST, preferred_element_type=jnp.float32)
+
+    for group in (tok_copies, ret_copies, rs_copies, sm_copies, in_copies):
+        for copy in group.values():
+            copy.wait_send()
+
+
+def finish_block(grad_ref, scaled_ref, recip_ref, solved_ref, out_ref, right):
+    @pl.when(pl.program_id(0) == 0)
+    def _():
+        v_high, v_low = split(solved_ref[...])
+        right[...] = jnp.concatenate([v_high, v_low, v_high, v_low], axis=0)
+
+    s_high, s_low = split(scaled_ref[...])
+    left = jnp.concatenate([s_high, s_high, s_low, s_low], axis=0)
+    fix = f32_dot(left, right[...], ((0,), (0,)))
+    scale = recip_ref[...].T[:, :1]
+    out_ref[...] = grad_ref[...] * scale - fix
+
+
+def fast(sizes, tokens, routing, gate_values, expert_weight, subspace, gradient):
+    n_dp, n_exp = sizes["dp"], sizes["expert"]
+    rows, width = tokens.shape
+    choices = routing.shape[1]
+    cap = rows * choices // n_exp * 9 // 8
+    cap = -(-cap // 8) * 8
+    rank = subspace.shape[1]
+    hidden = expert_weight.shape[2]
+    half = hidden // 2
+    chunk = width // n_dp
+    token_mean = float(rows * choices * n_dp)
+    f32, b16 = jnp.float32, jnp.bfloat16
+    hbm = pl.BlockSpec(memory_space=pl.ANY)
+    vmem = pl.BlockSpec(memory_space=pltpu.VMEM)
+    dma = pltpu.SemaphoreType.DMA
+    combined, basis, solved, scaled, recip = pl.pallas_call(
+        functools.partial(exchange, n_dp, n_exp, cap, token_mean),
+        out_shape=(
+            jax.ShapeDtypeStruct((rows, half), b16),
+            jax.ShapeDtypeStruct((rank, chunk), f32),
+            jax.ShapeDtypeStruct((rank, hidden), f32),
+            jax.ShapeDtypeStruct((rank, chunk), f32),
+            jax.ShapeDtypeStruct((8, chunk), f32),
+        ),
+        in_specs=[hbm, vmem, vmem, hbm, hbm, hbm],
+        out_specs=(vmem,) * 5,
+        scratch_shapes=[
+            pltpu.VMEM((rows, width), b16),
+            pltpu.VMEM((rank, width), b16),
+            pltpu.VMEM((width, hidden), b16),
+            pltpu.VMEM((chunk, hidden), f32),
+            pltpu.VMEM((chunk, hidden), b16),
+            pltpu.VMEM((chunk, hidden), b16),
+            pltpu.VMEM((n_exp - 1, cap, width), b16),
+            pltpu.VMEM((n_exp, cap, width), b16),
+            pltpu.VMEM((n_exp, 2, cap, half), b16),
+            pltpu.VMEM((n_exp, 2, cap, half), b16),
+            pltpu.VMEM((n_dp, rank + 8, chunk), f32),
+            pltpu.VMEM((n_dp, rank + 8, chunk), f32),
+            pltpu.VMEM((rank, 2 * rank), f32),
+            pltpu.VMEM((n_dp, rank, 2 * rank), f32),
+            pltpu.VMEM((rank, hidden), f32),
+            pltpu.VMEM((n_dp, rank, hidden), f32),
+            pltpu.VMEM((rank, 2 * rank), f32),
+            dma((4,)), dma((n_exp,)), dma((n_exp,)), dma((n_exp, 2)), dma((n_exp, 2)),
+            dma((n_dp,)), dma((n_dp,)), dma((n_dp,)), dma((n_dp,)), dma((n_dp,)), dma((n_dp,)),
+        ],
+        compiler_params=pltpu.CompilerParams(
+            collective_id=0, has_side_effects=True, vmem_limit_bytes=48 * 1024 * 1024
+        ),
+    )(tokens, routing.T, gate_values.T, expert_weight[0], subspace[0], gradient[0, 0])
+    block = 128
+    result = pl.pallas_call(
+        finish_block,
+        grid=(chunk // block,),
+        out_shape=jax.ShapeDtypeStruct((chunk, hidden), f32),
+        in_specs=[
+            pl.BlockSpec((block, hidden), lambda i: (i, 0)),
+            pl.BlockSpec((rank, block), lambda i: (0, i)),
+            pl.BlockSpec((8, block), lambda i: (0, i)),
+            pl.BlockSpec((rank, hidden), lambda i: (0, 0)),
+        ],
+        out_specs=pl.BlockSpec((block, hidden), lambda i: (i, 0)),
+        scratch_shapes=[pltpu.VMEM((4 * rank, hidden), b16)],
+    )(gradient[0, 0], scaled, recip, solved)
+    return (combined, basis[None, None], result[None, None])
+
+
 def solution(mesh):
     in_specs = (
         P(("dp", "expert"), "tensor"),
@@ -105,4 +418,11 @@
         P("expert", "tensor", None, "dp"),
         P("expert", "tensor", "dp", None),
     )
-    return jax.shard_map(body, mesh=mesh, in_specs=in_specs, out_specs=out_specs, check_vma=False)
+
+    def run(tokens, routing, gate_values, expert_weight, subspace, gradient):
+        sizes = dict(mesh.shape)
+        if fits(sizes, tokens, subspace, gradient, expert_weight):
+            return fast(sizes, tokens, routing, gate_values, expert_weight, subspace, gradient)
+        return body(tokens, routing, gate_values, expert_weight, subspace, gradient)
+
+    return jax.shard_map(run, mesh=mesh, in_specs=in_specs, out_specs=out_specs, check_vma=False)

time: 206 us -> 110 us (0.53)
  Pallas kernels: 0 us -> 99.6 us
  blocking collectives: 74.8 us -> 0 us
  waiting for transfers between devices: 48.9 us -> 0 us
  matrix products: 29.4 us -> 0 us
  other arithmetic: 29.2 us -> 0 us
  between operations: 14.2 us -> 0.66 us
  local copies, waits for them, and re-layouts: 5.3 us -> 8.91 us
  starting transfers between devices: 3.56 us -> 0 us
    pallas_call x0 -> x2, Pallas kernels: none -> 99.6 us  [the longest x1 92.5 us: fast(): pl.pallas_call(functools.partial(exchange, n_dp, n_exp, cap, token_mean),...]
    all_to_all x2 -> x0, blocking collectives: 57.9 us -> none  [the longest x1 53.6 us: body(): lax.all_to_all(outgoing, 'expert', split_axis=0, concat_axis=0, tiled=True)]
    psum x1 -> x0, waiting for transfers between devices: 33.8 us -> none  [body(): lax.psum((gram_part, curve_part, inner_part), 'dp')]
    dot_general x10 -> x0, matrix products: 26.7 us -> none  [the longest x1 6.19 us: body(): jnp.dot(slab_rows, expert_weight[0], preferred_element_type=jnp.float32)]
    another operation x10 -> x0, other arithmetic: 24.1 us -> none  [the longest x4 11.1 us: tri_solve(): lax.linalg.triangular_solve(factor, rhs, left_side=True, lower=True, tran...]
    psum x1 -> x0, blocking collectives: 17 us -> none  [body(): lax.psum((gram_part, curve_part, inner_part), 'dp')]
    all_to_all x1 -> x0, waiting for transfers between devices: 15 us -> none  [body(): lax.all_to_all(shaped, 'expert', split_axis=0, concat_axis=0, tiled=True)]
    unnamed x5 -> x18, local copies, waits for them, and re-layouts: 0.88 us -> 8.91 us
  transfers between devices with their start and end apart: 3 -> 0, of which waited for: 2 -> 0; matrix products, arithmetic and copies ran while one was open for 8% -> 0% of each run, Pallas kernels for 0% -> 0%
where the time goes in v1:
time: 110 us; the launch traced here: 109 us
  Pallas kernels  99.6 us (91%)
  local copies, waits for them, and re-layouts  8.91 us (8%)
    pallas_call x1, Pallas kernels, fast(): pl.pallas_call(functools.partial(exchange, n_dp, n_exp, cap, token_mean),...  92.5 us
    unnamed x18, local copies, waits for them, and re-layouts  8.91 us
    pallas_call x1, Pallas kernels, fast(): pl.pallas_call(finish_block, grid=(chunk // block,), out_shape=jax.ShapeD...  7.1 us

profile of v1, /device:TPU:0, one launch (start us, length us, event | category | flops | bytes accessed | tf_op | source)
XLA Modules:
  0.0 109.2 jit_solution(8319010670930311589)
XLA Ops:
  0.6 0.0 copy-start
  0.6 2.0 %copy-done = f32[1,1,896,1024]{3,2,1,0:T(8,128)S(1)} copy-done((f32[1,1,896,1024]{3,2,1,0:T(8,128)S(1)}, f32[1,1,896,1024]{3,2,1,0:T(8,128)}, u32[]{:S(2)}) %copy-start) | copy-done | bytes 3670040
  2.7 0.0 copy-start.1
  2.7 1.2 %copy-done.1 = bf16[128,3584]{1,0:T(8,128)(2,1)S(1)} copy-done((bf16[128,3584]{1,0:T(8,128)(2,1)S(1)}, bf16[128,3584]{1,0:T(8,128)(2,1)}, u32[]{:S(2)}) %copy-start.1) | copy-done | bytes 917528
  3.9 0.0 copy-start.2
  3.9 1.0 copy-done.2
  4.9 0.0 copy-start.6
  4.9 0.7 copy-done.6
  5.6 0.0 copy-start.7
  5.6 0.7 copy-done.7
  6.2 92.5 %shard_map.85 = (bf16[128,512]{1,0:T(8,128)(2,1)S(1)}, f32[64,896]{1,0:T(8,128)S(1)}, f32[64,1024]{1,0:T(8,128)S(1)}, f32[64,896]{1,0:T(8,128)S(1)}, f32[8,896]{1,0:T(8,128)S(1)}) custom-call(bf16[128,3584]{1,0:T(8,128)(2,1)S(1)} %copy-done.1, s32[2,128]{1,0:T(2,128)S(1)} %bitcast.11, f32[2,128]{1,0:T(2,128)S(1)} %bitcast.12, bf16[3584,1024]{1,0:T(8,128)(2,1)} %bitcast.13, ...), custom_call_target="tpu_custom_call" | custom-call | tf_op jit(solution)/shard_map/pallas_call | solution.py:354
  98.8 0.0 copy-start.3
  98.8 0.7 copy-done.3
  99.4 0.0 copy-start.4
  99.4 0.7 copy-done.4
  100.1 0.0 copy-start.5
  100.1 0.6 copy-done.5
  100.7 7.1 %shard_map.86 = f32[896,1024]{1,0:T(8,128)} custom-call(f32[896,1024]{1,0:T(8,128)} %bitcast.7, f32[64,896]{1,0:T(8,128)} %copy-done.4, f32[8,896]{1,0:T(8,128)} %copy-done.5, f32[64,1024]{1,0:T(8,128)} %copy-done.3), custom_call_target="tpu_custom_call" | custom-call | tf_op jit(solution)/shard_map/pallas_call | solution.py:391
  107.8 0.7 copy.11
  108.5 0.7 copy.12
Async XLA Ops:
  0.6 2.0 %copy-start = (f32[1,1,896,1024]{3,2,1,0:T(8,128)S(1)}, f32[1,1,896,1024]{3,2,1,0:T(8,128)}, u32[]{:S(2)}) copy-start(f32[1,1,896,1024]{3,2,1,0:T(8,128)} %param.11) | copy-start | bytes 11010052
  2.7 1.2 %copy-start.1 = (bf16[128,3584]{1,0:T(8,128)(2,1)S(1)}, bf16[128,3584]{1,0:T(8,128)(2,1)}, u32[]{:S(2)}) copy-start(bf16[128,3584]{1,0:T(8,128)(2,1)} %tok_hbm.1) | copy-start | bytes 2752516
  3.9 1.0 copy-start.2
  4.9 0.7 copy-start.6
  5.6 0.7 copy-start.7
  98.8 0.7 copy-start.3
  99.4 0.7 copy-start.4
  100.1 0.6 copy-start.5

commit v2 on v1

--- a/solution.py
+++ b/solution.py
@@ -104,8 +104,8 @@
 
 
 def fits(sizes, tokens, subspace, gradient, expert_weight):
-    few = sizes["dp"] <= 4 and sizes["expert"] <= 4 and sizes["tensor"] == 2
-    even = is_power(sizes["dp"]) and is_power(sizes["expert"])
+    few = sizes["dp"] == 4 and sizes["expert"] <= 4 and sizes["tensor"] == 2
+    even = is_power(sizes["expert"])
     lanes = gradient.shape[2] % 128 == 0 and expert_weight.shape[2] % 256 == 0
     return few and even and lanes and subspace.shape[1] == 64 and tokens.shape[0] == 128
 
@@ -129,30 +129,34 @@
     return lax.dot_general(a, b, (dims, ((), ())), preferred_element_type=jnp.float32)
 
 
-def eliminate(matrix, work):
+def eliminate(matrix):
     rank = matrix.shape[0]
     row_id = lax.broadcasted_iota(jnp.int32, (rank, 2 * rank), 0)
-    lane_id = lax.broadcasted_iota(jnp.int32, (rank, 2 * rank), 1)
     eye = (lax.broadcasted_iota(jnp.int32, (rank, rank), 0) == lax.broadcasted_iota(jnp.int32, (rank, rank), 1)).astype(jnp.float32)
-    work[...] = jnp.concatenate([matrix, eye], axis=1)
-
-    def step(j, state):
-        row = work[pl.ds(j, 1), :]
-        pivot = jnp.sum(jnp.where(lane_id[:1] == j, row, 0.0), axis=1, keepdims=True)
-        column = jnp.sum(jnp.where(lane_id == j, state, 0.0), axis=1, keepdims=True)
-        factor = jnp.where(row_id[:, :1] > j, column, 0.0) / pivot
-        state = state - factor * row
-        work[...] = state
-        return state
-
-    state = lax.fori_loop(0, rank, step, work[...])
+    state = jnp.concatenate([matrix, eye], axis=1)
+    group = 8
+    for j in range(0, rank, group):
+        cols = [jnp.broadcast_to(state[:, j + i:j + i + 1], (rank, 2 * rank)) for i in range(group)]
+        rows = [state[j + i:j + i + 1, :] for i in range(group)]
+        delta = None
+        for i in range(group):
+            inverse = 1.0 / cols[i][j + i:j + i + 1, :]
+            factor = jnp.where(row_id > j + i, cols[i] * inverse, 0.0)
+            for m in range(i + 1, group):
+                ratio = cols[i][j + m:j + m + 1, :] * inverse
+                rows[m] = rows[m] - ratio * rows[i]
+                cols[m] = cols[m] - cols[i] * ratio
+            term = factor * rows[i]
+            delta = term if delta is None else delta + term
+        state = state - delta
     return state[:, :rank], state[:, rank:], jnp.sum(state[:, :rank] * eye, axis=1, keepdims=True)
 
 
-def exchange(n_dp, n_exp, cap, token_mean, tok_hbm, route_ref, gate_ref, w_hbm, sub_hbm, grad_hbm,
-             comb_ref, basis_ref, solved_ref, scaled_ref, recip_ref,
-             tok, sub, wgt, grad, g_high, g_low, out_rows, in_rows, parts, ret, image, rs_in, small, small_in,
-             inner, inner_in, work, loc_sem, tok_s, tok_r, ret_s, ret_r, rs_s, rs_r, sm_s, sm_r, in_s, in_r):
+def exchange(n_dp, n_exp, cap, token_mean, tok_hbm, route_hbm, gate_hbm, w_hbm, sub_hbm, grad_hbm,
+             comb_hbm, basis_hbm, result_hbm,
+             tok, route_ref, gate_ref, sub, wgt, grad, g_high, g_low, out_rows, in_rows, parts, ret, image, forward, rs_in,
+             small, small_in, inner, inner_mid, inner_in, left, comb, basis,
+             loc_sem, out_sem, tok_s, tok_r, ret_s, ret_r, rs_s, rs_r, sm_s, sm_r, in_s, in_r):
     dp = lax.axis_index("dp")
     ex = lax.axis_index("expert")
     core = lax.axis_index("tensor")
@@ -161,15 +165,18 @@
     chunk = width // n_dp
     rank = sub.shape[0]
     rows = tok.shape[0]
+    cut = (rank + 8) // 16 * 8 + 8 * ((rank + 8) // 8 % 2)
 
     loads = [
         pltpu.make_async_copy(tok_hbm, tok, loc_sem.at[0]),
         pltpu.make_async_copy(sub_hbm, sub, loc_sem.at[1]),
         pltpu.make_async_copy(w_hbm, wgt, loc_sem.at[2]),
         pltpu.make_async_copy(grad_hbm, grad, loc_sem.at[3]),
+        pltpu.make_async_copy(route_hbm, route_ref, loc_sem.at[4]),
+        pltpu.make_async_copy(gate_hbm, gate_ref, loc_sem.at[5]),
     ]
-    for load in loads:
-        load.start()
+    for i in (4, 0, 1, 5, 2, 3):
+        loads[i].start()
 
     barrier = pltpu.get_barrier_semaphore()
     peers = [(dp, flip(ex, k, n_exp), core) for k in range(1, n_exp)]
@@ -182,6 +189,7 @@
     col_i = lax.broadcasted_iota(jnp.int32, (rows, rows), 1)
     earlier = (row_i < col_i).astype(jnp.float32)
     slot_i = lax.broadcasted_iota(jnp.int32, (cap, rows), 0)
+    loads[4].wait()
     named = []
     for k in range(n_exp):
         hit = route_ref[...] == flip(ex, k, n_exp)
@@ -256,15 +264,32 @@
         if k != order[-1]:
             project(k)
 
+    bounds = ((0, cut), (cut, rank + 8))
+    firsts = (1, 2)
     rs_copies = {}
-    for k in range(n_dp - 1, 0, -1):
-        to = flip(dp, k, n_dp)
-        rs_copies[k] = send(image.at[to], rs_in.at[k], rs_s.at[k], rs_r.at[k], (to, ex, core))
+    for turn in (0, 1):
+        for part in range(2):
+            lo, hi = bounds[part]
+            near = firsts[part]
+            to = flip(dp, near, n_dp)
+            which = flip(dp, 3, n_dp) if turn == 0 else to
+            rs_copies[part, turn] = send(
+                image.at[which, lo:hi], rs_in.at[turn, lo:hi], rs_s.at[part, turn], rs_r.at[part, turn], (to, ex, core)
+            )
     project(order[-1])
-    total = image[dp]
-    for k in range(1, n_dp):
-        rs_copies[k].wait_recv()
-        total = total + rs_in[k]
+    for part in range(2):
+        lo, hi = bounds[part]
+        far = 3 - firsts[part]
+        to = flip(dp, far, n_dp)
+        rs_copies[part, 0].wait_recv()
+        forward[lo:hi] = image[to, lo:hi] + rs_in[0, lo:hi]
+        rs_copies[part, 2] = send(
+            forward.at[lo:hi], rs_in.at[2, lo:hi], rs_s.at[part, 2], rs_r.at[part, 2], (to, ex, core)
+        )
+    for turn in (1, 2):
+        for part in range(2):
+            rs_copies[part, turn].wait_recv()
+    total = image[dp] + rs_in[1] + rs_in[2]
     mine = total[:rank]
     recip = 1.0 / (total[rank:rank + 1] / token_mean + EPSILON)
     scaled = mine * recip
@@ -278,24 +303,40 @@
     cross = f32_dot(s_both, g_high[...], ((1,), (0,)))
     inner[...] = cross[:rank] + cross[rank:] + f32_dot(s_high, g_low[...], ((1,), (0,)))
     in_copies = {}
-    for k in range(n_dp - 1, 0, -1):
-        in_copies[k] = send(inner, inner_in.at[k], in_s.at[k], in_r.at[k], (flip(dp, k, n_dp), ex, core))
-    scaled_ref[...] = scaled
-    recip_ref[...] = jnp.broadcast_to(recip, (8, chunk))
+    mid = rank // 2
+    for part in range(2):
+        rows_of = slice(part * mid, part * mid + mid)
+        in_copies[part, 0] = send(
+            inner.at[rows_of], inner_in.at[0, rows_of], in_s.at[part, 0], in_r.at[part, 0], (flip(dp, firsts[part], n_dp), ex, core)
+        )
+    left[...] = jnp.concatenate([s_high, s_high, s_low, s_low], axis=0).T
+    recip_cols = jnp.broadcast_to(recip, (8, chunk)).T
+    for c in range(0, chunk, 128):
+        grad[c:c + 128] = grad[c:c + 128] * recip_cols[c:c + 128, :1]
 
     sums = small[...]
     for k in range(1, n_dp):
         sm_copies[k].wait_recv()
         sums = sums + small_in[k]
-    upper, lower_inv, pivots = eliminate(sums[:, :rank], work)
+    upper, lower_inv, pivots = eliminate(sums[:, :rank])
+    for part in range(2):
+        rows_of = slice(part * mid, part * mid + mid)
+        in_copies[part, 0].wait_recv()
+        inner_mid[rows_of] = inner[rows_of] + inner_in[0, rows_of]
+        in_copies[part, 1] = send(
+            inner_mid.at[rows_of], inner_in.at[1, rows_of], in_s.at[part, 1], in_r.at[part, 1], (flip(dp, 3 - firsts[part], n_dp), ex, core)
+        )
     root = lax.rsqrt(pivots)
     transposed = upper * root
-    basis_ref[...] = root * lax.dot_general(lower_inv, mine, (((1,), (0,)), ((), ())), precision=HIGHEST, preferred_element_type=jnp.float32)
     middle = lax.dot_general(transposed * (root * token_mean), transposed, (((0,), (0,)), ((), ())), precision=HIGHEST, preferred_element_type=jnp.float32)
     middle = middle + sums[:, rank:]
-    _, mid_inv, mid_pivots = eliminate(middle, work)
+    _, mid_inv, mid_pivots = eliminate(middle)
     inverse = lax.dot_general(mid_inv / mid_pivots, mid_inv, (((0,), (0,)), ((), ())), precision=HIGHEST, preferred_element_type=jnp.float32)
-
+    basis[...] = root * lax.dot_general(lower_inv, mine, (((1,), (0,)), ((), ())), precision=HIGHEST, preferred_element_type=jnp.float32)
+    stores = [pltpu.make_async_copy(basis, basis_hbm, out_sem.at[0])]
+    stores[0].start()
+
+    loads[5].wait()
     gates = []
     for k in range(n_exp):
         hit = (route_ref[...] == flip(ex, k, n_exp)).astype(jnp.float32)
@@ -310,30 +351,27 @@
                 ret_copies[k, rel].wait_recv()
             hidden = hidden + f32_dot(pickers[k], ret[k, rel], ((0,), (0,)))
         combined = combined + gate_cols[:, k:k + 1] * hidden
-    comb_ref[...] = combined.astype(jnp.bfloat16)
-
-    inner_sum = inner[...]
-    for k in range(1, n_dp):
-        in_copies[k].wait_recv()
-        inner_sum = inner_sum + inner_in[k]
-    solved_ref[...] = lax.dot_general(inverse, inner_sum, (((1,), (0,)), ((), ())), precision=HIGHEST, preferred_element_type=jnp.float32)
+    comb[...] = combined.astype(jnp.bfloat16)
+    stores.append(pltpu.make_async_copy(comb, comb_hbm, out_sem.at[1]))
+    stores[1].start()
+
+    for part in range(2):
+        in_copies[part, 1].wait_recv()
+    inner_sum = inner_mid[...] + inner_in[1]
+    solved = lax.dot_general(inverse, inner_sum, (((1,), (0,)), ((), ())), precision=HIGHEST, preferred_element_type=jnp.float32)
+    v_high, v_low = split(solved)
+    right = jnp.concatenate([v_high, v_low, v_high, v_low], axis=0)
+    for c in range(0, chunk, 128):
+        grad[c:c + 128] = grad[c:c + 128] - f32_dot(left[c:c + 128], right, ((1,), (0,)))
+        store = pltpu.make_async_copy(grad.at[c:c + 128], result_hbm.at[c:c + 128], out_sem.at[2 + c // 128])
+        store.start()
+        stores.append(store)
 
     for group in (tok_copies, ret_copies, rs_copies, sm_copies, in_copies):
         for copy in group.values():
             copy.wait_send()
-
-
-def finish_block(grad_ref, scaled_ref, recip_ref, solved_ref, out_ref, right):
-    @pl.when(pl.program_id(0) == 0)
-    def _():
-        v_high, v_low = split(solved_ref[...])
-        right[...] = jnp.concatenate([v_high, v_low, v_high, v_low], axis=0)
-
-    s_high, s_low = split(scaled_ref[...])
-    left = jnp.concatenate([s_high, s_high, s_low, s_low], axis=0)
-    fix = f32_dot(left, right[...], ((0,), (0,)))
-    scale = recip_ref[...].T[:, :1]
-    out_ref[...] = grad_ref[...] * scale - fix
+    for store in stores:
+        store.wait()
 
 
 def fast(sizes, tokens, routing, gate_values, expert_weight, subspace, gradient):
@@ -351,19 +389,19 @@
     hbm = pl.BlockSpec(memory_space=pl.ANY)
     vmem = pl.BlockSpec(memory_space=pltpu.VMEM)
     dma = pltpu.SemaphoreType.DMA
-    combined, basis, solved, scaled, recip = pl.pallas_call(
+    combined, basis, result = pl.pallas_call(
         functools.partial(exchange, n_dp, n_exp, cap, token_mean),
         out_shape=(
             jax.ShapeDtypeStruct((rows, half), b16),
             jax.ShapeDtypeStruct((rank, chunk), f32),
-            jax.ShapeDtypeStruct((rank, hidden), f32),
-            jax.ShapeDtypeStruct((rank, chunk), f32),
-            jax.ShapeDtypeStruct((8, chunk), f32),
+            jax.ShapeDtypeStruct((chunk, hidden), f32),
         ),
-        in_specs=[hbm, vmem, vmem, hbm, hbm, hbm],
-        out_specs=(vmem,) * 5,
+        in_specs=[hbm] * 6,
+        out_specs=(hbm,) * 3,
         scratch_shapes=[
             pltpu.VMEM((rows, width), b16),
+            pltpu.VMEM((choices, rows), jnp.int32),
+            pltpu.VMEM((choices, rows), f32),
             pltpu.VMEM((rank, width), b16),
             pltpu.VMEM((width, hidden), b16),
             pltpu.VMEM((chunk, hidden), f32),
@@ -374,33 +412,23 @@
             pltpu.VMEM((n_exp, 2, cap, half), b16),
             pltpu.VMEM((n_exp, 2, cap, half), b16),
             pltpu.VMEM((n_dp, rank + 8, chunk), f32),
-            pltpu.VMEM((n_dp, rank + 8, chunk), f32),
+            pltpu.VMEM((rank + 8, chunk), f32),
+            pltpu.VMEM((3, rank + 8, chunk), f32),
             pltpu.VMEM((rank, 2 * rank), f32),
             pltpu.VMEM((n_dp, rank, 2 * rank), f32),
             pltpu.VMEM((rank, hidden), f32),
-            pltpu.VMEM((n_dp, rank, hidden), f32),
-            pltpu.VMEM((rank, 2 * rank), f32),
-            dma((4,)), dma((n_exp,)), dma((n_exp,)), dma((n_exp, 2)), dma((n_exp, 2)),
-            dma((n_dp,)), dma((n_dp,)), dma((n_dp,)), dma((n_dp,)), dma((n_dp,)), dma((n_dp,)),
+            pltpu.VMEM((rank, hidden), f32),
+            pltpu.VMEM((2, rank, hidden), f32),
+            pltpu.VMEM((chunk, 4 * rank), b16),
+            pltpu.VMEM((rows, half), b16),
+            pltpu.VMEM((rank, chunk), f32),
+            dma((6,)), dma((2 + chunk // 128,)), dma((n_exp,)), dma((n_exp,)), dma((n_exp, 2)), dma((n_exp, 2)),
+            dma((2, 3)), dma((2, 3)), dma((n_dp,)), dma((n_dp,)), dma((2, 2)), dma((2, 2)),
         ],
         compiler_params=pltpu.CompilerParams(
-            collective_id=0, has_side_effects=True, vmem_limit_bytes=48 * 1024 * 1024
+            collective_id=0, has_side_effects=True, vmem_limit_bytes=67000000
         ),
     )(tokens, routing.T, gate_values.T, expert_weight[0], subspace[0], gradient[0, 0])
-    block = 128
-    result = pl.pallas_call(
-        finish_block,
-        grid=(chunk // block,),
-        out_shape=jax.ShapeDtypeStruct((chunk, hidden), f32),
-        in_specs=[
-            pl.BlockSpec((block, hidden), lambda i: (i, 0)),
-            pl.BlockSpec((rank, block), lambda i: (0, i)),
-            pl.BlockSpec((8, block), lambda i: (0, i)),
-            pl.BlockSpec((rank, hidden), lambda i: (0, 0)),
-        ],
-        out_specs=pl.BlockSpec((block, hidden), lambda i: (i, 0)),
-        scratch_shapes=[pltpu.VMEM((4 * rank, hidden), b16)],
-    )(gradient[0, 0], scaled, recip, solved)
     return (combined, basis[None, None], result[None, None])
 
 

time: 110 us -> 89.1 us (0.81)
  Pallas kernels: 99.6 us -> 80.7 us
  local copies, waits for them, and re-layouts: 8.91 us -> 7.58 us
    pallas_call x1, Pallas kernels: 92.5 us -> 80.7 us  [fast(): pl.pallas_call(functools.partial(exchange, n_dp, n_exp, cap, token_mean),...]
    pallas_call x1 -> x0, Pallas kernels: 7.1 us -> none  [fast(): pl.pallas_call(finish_block, grid=(chunk // block,), out_shape=jax.ShapeD...]
    unnamed x18 -> x3, local copies, waits for them, and re-layouts: 8.91 us -> 7.58 us
where the time goes in v2:
time: 89.1 us; the launch traced here: 88.9 us
  Pallas kernels  80.7 us (91%)
  local copies, waits for them, and re-layouts  7.58 us (9%)
    pallas_call x1, Pallas kernels, fast(): pl.pallas_call(functools.partial(exchange, n_dp, n_exp, cap, token_mean),...  80.7 us
    unnamed x3, local copies, waits for them, and re-layouts  7.58 us

profile of v2, /device:TPU:0, one launch (start us, length us, event | category | flops | bytes accessed | tf_op | source)
XLA Modules:
  0.0 88.9 jit_solution(17358516324586445963)
XLA Ops:
  0.6 80.7 %shard_map.85 = (bf16[128,512]{1,0:T(8,128)(2,1)}, f32[64,896]{1,0:T(8,128)}, f32[896,1024]{1,0:T(8,128)}) custom-call(bf16[128,3584]{1,0:T(8,128)(2,1)} %tok_hbm.1, s32[2,128]{1,0:T(2,128)} %bitcast.12, f32[2,128]{1,0:T(2,128)} %bitcast.13, bf16[3584,1024]{1,0:T(8,128)(2,1)} %bitcast.7, bf16[64,3584]{1,0:T(8,128)(2,1)} %bitcast.10, f32[896,1024]{1,0:T(8,128)} %bitcast.9), custom_call_target="tpu_custom_call" | custom-call | tf_op jit(solution)/shard_map/pallas_call | solution.py:392
  81.3 1.6 %copy.12 = bf16[128,512]{1,0:T(8,128)(2,1)} copy(bf16[128,512]{1,0:T(8,128)(2,1)} %get-tuple-element.12) | data formatting | bytes 262144
  82.9 1.6 %copy.13 = f32[1,1,64,896]{3,2,1,0:T(8,128)} copy(f32[1,1,64,896]{3,2,1,0:T(8,128)} %bitcast.11) | data formatting | bytes 458752
  84.5 4.4 %copy.14 = f32[1,1,896,1024]{3,2,1,0:T(8,128)} copy(f32[1,1,896,1024]{3,2,1,0:T(8,128)} %bitcast.8) | data formatting | bytes 7340032

commit v3 on v2

--- a/solution.py
+++ b/solution.py
@@ -153,9 +153,9 @@
 
 
 def exchange(n_dp, n_exp, cap, token_mean, tok_hbm, route_hbm, gate_hbm, w_hbm, sub_hbm, grad_hbm,
-             comb_hbm, basis_hbm, result_hbm,
+             comb_hbm, basis_hbm, left_hbm, recip_hbm, solved_hbm,
              tok, route_ref, gate_ref, sub, wgt, grad, g_high, g_low, out_rows, in_rows, parts, ret, image, forward, rs_in,
-             small, small_in, inner, inner_mid, inner_in, left, comb, basis,
+             small, small_in, inner, inner_mid, inner_in, left, comb, basis, recips, solved,
              loc_sem, out_sem, tok_s, tok_r, ret_s, ret_r, rs_s, rs_r, sm_s, sm_r, in_s, in_r):
     dp = lax.axis_index("dp")
     ex = lax.axis_index("expert")
@@ -310,9 +310,10 @@
             inner.at[rows_of], inner_in.at[0, rows_of], in_s.at[part, 0], in_r.at[part, 0], (flip(dp, firsts[part], n_dp), ex, core)
         )
     left[...] = jnp.concatenate([s_high, s_high, s_low, s_low], axis=0).T
-    recip_cols = jnp.broadcast_to(recip, (8, chunk)).T
-    for c in range(0, chunk, 128):
-        grad[c:c + 128] = grad[c:c + 128] * recip_cols[c:c + 128, :1]
+    recips[...] = jnp.broadcast_to(recip, (8, chunk))
+    stores = [pltpu.make_async_copy(left, left_hbm, out_sem.at[2]), pltpu.make_async_copy(recips, recip_hbm, out_sem.at[3])]
+    for store in stores:
+        store.start()
 
     sums = small[...]
     for k in range(1, n_dp):
@@ -333,8 +334,8 @@
     _, mid_inv, mid_pivots = eliminate(middle)
     inverse = lax.dot_general(mid_inv / mid_pivots, mid_inv, (((0,), (0,)), ((), ())), precision=HIGHEST, preferred_element_type=jnp.float32)
     basis[...] = root * lax.dot_general(lower_inv, mine, (((1,), (0,)), ((), ())), precision=HIGHEST, preferred_element_type=jnp.float32)
-    stores = [pltpu.make_async_copy(basis, basis_hbm, out_sem.at[0])]
-    stores[0].start()
+    stores.append(pltpu.make_async_copy(basis, basis_hbm, out_sem.at[0]))
+    stores[2].start()
 
     loads[5].wait()
     gates = []
@@ -353,23 +354,47 @@
         combined = combined + gate_cols[:, k:k + 1] * hidden
     comb[...] = combined.astype(jnp.bfloat16)
     stores.append(pltpu.make_async_copy(comb, comb_hbm, out_sem.at[1]))
-    stores[1].start()
+    stores[3].start()
 
     for part in range(2):
         in_copies[part, 1].wait_recv()
     inner_sum = inner_mid[...] + inner_in[1]
-    solved = lax.dot_general(inverse, inner_sum, (((1,), (0,)), ((), ())), precision=HIGHEST, preferred_element_type=jnp.float32)
-    v_high, v_low = split(solved)
-    right = jnp.concatenate([v_high, v_low, v_high, v_low], axis=0)
-    for c in range(0, chunk, 128):
-        grad[c:c + 128] = grad[c:c + 128] - f32_dot(left[c:c + 128], right, ((1,), (0,)))
-        store = pltpu.make_async_copy(grad.at[c:c + 128], result_hbm.at[c:c + 128], out_sem.at[2 + c // 128])
-        store.start()
-        stores.append(store)
-
+    solved[...] = lax.dot_general(inverse, inner_sum, (((1,), (0,)), ((), ())), precision=HIGHEST, preferred_element_type=jnp.float32)
+    stores.append(pltpu.make_async_copy(solved, solved_hbm, out_sem.at[4]))
+    stores[4].start()
     for group in (tok_copies, ret_copies, rs_copies, sm_copies, in_copies):
         for copy in group.values():
             copy.wait_send()
+    for store in stores:
+        store.wait()
+
+
+def apply(grad_hbm, left_hbm, recip_hbm, solved_hbm, comb_hbm, basis_hbm, comb_out, basis_out, result_hbm,
+          grad, left, recips, solved, comb, basis, sem, out_sem):
+    chunk = grad.shape[0]
+    block = 128
+    small = [(solved_hbm, solved), (recip_hbm, recips), (left_hbm, left), (comb_hbm, comb), (basis_hbm, basis)]
+    loads = [pltpu.make_async_copy(src, dst, sem.at[i]) for i, (src, dst) in enumerate(small)]
+    for c in range(0, chunk, block):
+        loads.append(pltpu.make_async_copy(grad_hbm.at[c:c + block], grad.at[c:c + block], sem.at[len(loads)]))
+    for load in loads:
+        load.start()
+    loads[0].wait()
+    v_high, v_low = split(solved[...])
+    right = jnp.concatenate([v_high, v_low, v_high, v_low], axis=0)
+    loads[1].wait()
+    recip_cols = recips[...].T
+    loads[2].wait()
+    stores = []
+    for i, c in enumerate(range(0, chunk, block)):
+        loads[5 + i].wait()
+        grad[c:c + block] = grad[c:c + block] * recip_cols[c:c + block, :1] - f32_dot(left[c:c + block], right, ((1,), (0,)))
+        stores.append(pltpu.make_async_copy(grad.at[c:c + block], result_hbm.at[c:c + block], out_sem.at[i]))
+        stores[-1].start()
+    for i, (src, dst) in enumerate(((comb, comb_out), (basis, basis_out))):
+        loads[3 + i].wait()
+        stores.append(pltpu.make_async_copy(src, dst, out_sem.at[chunk // block + i]))
+        stores[-1].start()
     for store in stores:
         store.wait()
 
@@ -389,15 +414,17 @@
     hbm = pl.BlockSpec(memory_space=pl.ANY)
     vmem = pl.BlockSpec(memory_space=pltpu.VMEM)
     dma = pltpu.SemaphoreType.DMA
-    combined, basis, result = pl.pallas_call(
+    combined, basis, left, recip, solved = pl.pallas_call(
         functools.partial(exchange, n_dp, n_exp, cap, token_mean),
         out_shape=(
             jax.ShapeDtypeStruct((rows, half), b16),
             jax.ShapeDtypeStruct((rank, chunk), f32),
-            jax.ShapeDtypeStruct((chunk, hidden), f32),
+            jax.ShapeDtypeStruct((chunk, 4 * rank), b16),
+            jax.ShapeDtypeStruct((8, chunk), f32),
+            jax.ShapeDtypeStruct((rank, hidden), f32),
         ),
         in_specs=[hbm] * 6,
-        out_specs=(hbm,) * 3,
+        out_specs=(hbm,) * 5,
         scratch_shapes=[
             pltpu.VMEM((rows, width), b16),
             pltpu.VMEM((choices, rows), jnp.int32),
@@ -422,13 +449,35 @@
             pltpu.VMEM((chunk, 4 * rank), b16),
             pltpu.VMEM((rows, half), b16),
             pltpu.VMEM((rank, chunk), f32),
-            dma((6,)), dma((2 + chunk // 128,)), dma((n_exp,)), dma((n_exp,)), dma((n_exp, 2)), dma((n_exp, 2)),
+            pltpu.VMEM((8, chunk), f32),
+            pltpu.VMEM((rank, hidden), f32),
+            dma((6,)), dma((5,)), dma((n_exp,)), dma((n_exp,)), dma((n_exp, 2)), dma((n_exp, 2)),
             dma((2, 3)), dma((2, 3)), dma((n_dp,)), dma((n_dp,)), dma((2, 2)), dma((2, 2)),
         ],
         compiler_params=pltpu.CompilerParams(
             collective_id=0, has_side_effects=True, vmem_limit_bytes=67000000
         ),
     )(tokens, routing.T, gate_values.T, expert_weight[0], subspace[0], gradient[0, 0])
+    combined, basis, result = pl.pallas_call(
+        apply,
+        out_shape=(
+            jax.ShapeDtypeStruct((rows, half), b16),
+            jax.ShapeDtypeStruct((rank, chunk), f32),
+            jax.ShapeDtypeStruct((chunk, hidden), f32),
+        ),
+        in_specs=[hbm] * 6,
+        out_specs=(hbm,) * 3,
+        scratch_shapes=[
+            pltpu.VMEM((chunk, hidden), f32),
+            pltpu.VMEM((chunk, 4 * rank), b16),
+            pltpu.VMEM((8, chunk), f32),
+            pltpu.VMEM((rank, hidden), f32),
+            pltpu.VMEM((rows, half), b16),
+            pltpu.VMEM((rank, chunk), f32),
+            dma((5 + chunk // 128,)), dma((2 + chunk // 128,)),
+        ],
+        compiler_params=pltpu.CompilerParams(vmem_limit_bytes=67000000),
+    )(gradient[0, 0], left, recip, solved, combined, basis)
     return (combined, basis[None, None], result[None, None])
 
 

time: 89.1 us -> 84.2 us (0.945)
  local copies, waits for them, and re-layouts: 7.58 us -> 0 us
  Pallas kernels: 80.7 us -> 83.4 us
    unnamed x3 -> x0, local copies, waits for them, and re-layouts: 7.58 us -> none
    pallas_call x0 -> x1, Pallas kernels: none -> 4.13 us  [fast(): pl.pallas_call(apply, out_shape=(jax.ShapeDtypeStruct((rows, half), b16),...]
    pallas_call x1, Pallas kernels: 80.7 us -> 79.3 us  [fast(): pl.pallas_call(functools.partial(exchange, n_dp, n_exp, cap, token_mean),...]
where the time goes in v3:
time: 84.2 us; the launch traced here: 84.1 us
  Pallas kernels  83.4 us (99%)
    pallas_call x1, Pallas kernels, fast(): pl.pallas_call(functools.partial(exchange, n_dp, n_exp, cap, token_mean),...  79.3 us
    pallas_call x1, Pallas kernels, fast(): pl.pallas_call(apply, out_shape=(jax.ShapeDtypeStruct((rows, half), b16),...  4.13 us

profile of v3, /device:TPU:0, one launch (start us, length us, event | category | flops | bytes accessed | tf_op | source)
XLA Modules:
  0.0 84.1 jit_solution(17556448848123720059)
XLA Ops:
  0.6 79.3 %shard_map.85 = (bf16[128,512]{1,0:T(8,128)(2,1)}, f32[64,896]{1,0:T(8,128)}, bf16[896,256]{1,0:T(8,128)(2,1)}, f32[8,896]{1,0:T(8,128)}, f32[64,1024]{1,0:T(8,128)}) custom-call(bf16[128,3584]{1,0:T(8,128)(2,1)} %tok_hbm.1, s32[2,128]{1,0:T(2,128)} %bitcast.11, f32[2,128]{1,0:T(2,128)} %bitcast.12, bf16[3584,1024]{1,0:T(8,128)(2,1)} %bitcast.9, ...), custom_call_target="tpu_custom_call" | custom-call | tf_op jit(solution)/shard_map/pallas_call | solution.py:417
  79.9 4.1 %shard_map.86 = (bf16[128,512]{1,0:T(8,128)(2,1)}, f32[64,896]{1,0:T(8,128)}, f32[896,1024]{1,0:T(8,128)}) custom-call(f32[896,1024]{1,0:T(8,128)} %bitcast.8, bf16[896,256]{1,0:T(8,128)(2,1)} %get-tuple-element.11.left_hbm, f32[8,896]{1,0:T(8,128)} %get-tuple-element.12.recip_hbm, f32[64,1024]{1,0:T(8,128)} %get-tuple-element.13.solved_hbm, ...), custom_call_target="tpu_custom_call" | custom-call | tf_op jit(solution)/shard_map/pallas_call | solution.py:461

commit v4 on v3

--- a/solution.py
+++ b/solution.py
@@ -104,7 +104,7 @@
 
 
 def fits(sizes, tokens, subspace, gradient, expert_weight):
-    few = sizes["dp"] == 4 and sizes["expert"] <= 4 and sizes["tensor"] == 2
+    few = sizes["dp"] == 4 and sizes["expert"] == 4 and sizes["tensor"] == 2
     even = is_power(sizes["expert"])
     lanes = gradient.shape[2] % 128 == 0 and expert_weight.shape[2] % 256 == 0
     return few and even and lanes and subspace.shape[1] == 64 and tokens.shape[0] == 128
@@ -156,7 +156,9 @@
              comb_hbm, basis_hbm, left_hbm, recip_hbm, solved_hbm,
              tok, route_ref, gate_ref, sub, wgt, grad, g_high, g_low, out_rows, in_rows, parts, ret, image, forward, rs_in,
              small, small_in, inner, inner_mid, inner_in, left, comb, basis, recips, solved,
-             loc_sem, out_sem, tok_s, tok_r, ret_s, ret_r, rs_s, rs_r, sm_s, sm_r, in_s, in_r):
+             out_last, in_last, fwd_in, p_out, p_in,
+             loc_sem, out_sem, tok_s, tok_r, ret_s, ret_r, rs_s, rs_r, sm_s, sm_r, in_s, in_r,
+             last_s, last_r, fwd_s, fwd_r, p_s, p_r):
     dp = lax.axis_index("dp")
     ex = lax.axis_index("expert")
     core = lax.axis_index("tensor")
@@ -215,9 +217,21 @@
         return copy
 
     tok_copies = {}
+    last = n_exp // 2
+    turns = (3, 1, 2, 0)
+    last_copies, fwd_copies, p_copies = {}, {}, {}
+
+    def columns(kd):
+        return pl.ds(pl.multiple_of(flip(dp, kd, n_dp) * chunk, 128), chunk)
+
     for k in list(range(n_exp - 1, 0, -1)):
-        out_rows[k - 1] = f32_dot(pickers[k], tok[...], ((1,), (0,))).astype(jnp.bfloat16)
-        tok_copies[k] = send(out_rows.at[k - 1], in_rows.at[k], tok_s.at[k], tok_r.at[k], (dp, flip(ex, k, n_exp), core))
+        if k == last:
+            for kd in turns:
+                out_last[kd] = f32_dot(pickers[k], tok[:, columns(kd)], ((1,), (0,))).astype(jnp.bfloat16)
+                last_copies[kd] = send(out_last.at[kd], in_last.at[kd], last_s.at[kd], last_r.at[kd], (dp, flip(ex, k, n_exp), core))
+            continue
+        out_rows[k // 2] = f32_dot(pickers[k], tok[...], ((1,), (0,))).astype(jnp.bfloat16)
+        tok_copies[k] = send(out_rows.at[k // 2], in_rows.at[k], tok_s.at[k], tok_r.at[k], (dp, flip(ex, k, n_exp), core))
     in_rows[0] = f32_dot(pickers[0], tok[...], ((1,), (0,))).astype(jnp.bfloat16)
     loads[1].wait()
 
@@ -257,7 +271,7 @@
     high, low = split(grad[...])
     g_high[...] = high
     g_low[...] = low
-    order = list(range(1, n_exp))
+    order = [k for k in range(1, n_exp) if k != last]
     for k in order:
         tok_copies[k].wait_recv()
         add_image(k)
@@ -286,12 +300,47 @@
         rs_copies[part, 2] = send(
             forward.at[lo:hi], rs_in.at[2, lo:hi], rs_s.at[part, 2], rs_r.at[part, 2], (to, ex, core)
         )
+
+    half_cols = [pl.ds(pl.multiple_of((core if rel == 0 else 1 - core) * half, half), half) for rel in range(2)]
+    projected = jnp.zeros((cap, rank), jnp.float32)
+    sums2 = [jnp.zeros((cap, half), jnp.float32) for _ in range(2)]
+
+    def add_products(kd):
+        at = pl.ds(pl.multiple_of(flip(dp, kd, n_dp) * chunk, 128), chunk)
+        for rel in range(2):
+            sums2[rel] = sums2[rel] + f32_dot(in_last[kd], wgt[at, half_cols[rel]], ((1,), (0,)))
+
+    for kd in turns:
+        last_copies[kd].wait_recv()
+        if kd:
+            fwd_copies[kd] = send(in_last.at[kd], fwd_in.at[kd], fwd_s.at[kd], fwd_r.at[kd], (flip(dp, kd, n_dp), ex, core))
+        projected = projected + f32_dot(in_last[kd], sub[:, columns(kd)], ((1,), (1,)))
+        if kd != turns[-1]:
+            add_products(kd)
+    p_out[...] = jnp.concatenate([projected, jnp.zeros((cap, 128 - rank), jnp.float32)], axis=1).astype(jnp.bfloat16)
+    for kd in range(n_dp - 1, 0, -1):
+        p_copies[kd] = send(p_out, p_in.at[kd], p_s.at[kd], p_r.at[kd], (flip(dp, kd, n_dp), ex, core))
+    add_products(turns[-1])
+    for rel in range(2):
+        parts[last, rel] = sums2[rel].astype(jnp.bfloat16)
+        peer = (dp, flip(ex, last, n_exp), core if rel == 0 else 1 - core)
+        ret_copies[last, rel] = send(parts.at[last, rel], ret.at[last, rel], ret_s.at[last, rel], ret_r.at[last, rel], peer)
+
     for turn in (1, 2):
         for part in range(2):
             rs_copies[part, turn].wait_recv()
     total = image[dp] + rs_in[1] + rs_in[2]
     mine = total[:rank]
-    recip = 1.0 / (total[rank:rank + 1] / token_mean + EPSILON)
+    squares = total[rank:rank + 1]
+    for kd in range(n_dp):
+        if kd:
+            fwd_copies[kd].wait_recv()
+            p_copies[kd].wait_recv()
+        part_rows = fwd_in[kd] if kd else in_last[0]
+        mine = mine + f32_dot(p_in[kd] if kd else p_out[...], part_rows, ((0,), (0,)))[:rank]
+        wide = part_rows.astype(jnp.float32)
+        squares = squares + jnp.sum(wide * wide, axis=0, keepdims=True)
+    recip = 1.0 / (squares / token_mean + EPSILON)
     scaled = mine * recip
     both = jnp.concatenate([mine, scaled], axis=0)
     small[...] = lax.dot_general(mine, both, (((1,), (1,)), ((), ())), precision=HIGHEST, preferred_element_type=jnp.float32)
@@ -362,7 +411,7 @@
     solved[...] = lax.dot_general(inverse, inner_sum, (((1,), (0,)), ((), ())), precision=HIGHEST, preferred_element_type=jnp.float32)
     stores.append(pltpu.make_async_copy(solved, solved_hbm, out_sem.at[4]))
     stores[4].start()
-    for group in (tok_copies, ret_copies, rs_copies, sm_copies, in_copies):
+    for group in (last_copies, fwd_copies, p_copies, tok_copies, ret_copies, rs_copies, sm_copies, in_copies):
         for copy in group.values():
             copy.wait_send()
     for store in stores:
@@ -434,7 +483,7 @@
             pltpu.VMEM((chunk, hidden), f32),
             pltpu.VMEM((chunk, hidden), b16),
             pltpu.VMEM((chunk, hidden), b16),
-            pltpu.VMEM((n_exp - 1, cap, width), b16),
+            pltpu.VMEM((n_exp - 2, cap, width), b16),
             pltpu.VMEM((n_exp, cap, width), b16),
             pltpu.VMEM((n_exp, 2, cap, half), b16),
             pltpu.VMEM((n_exp, 2, cap, half), b16),
@@ -451,8 +500,14 @@
             pltpu.VMEM((rank, chunk), f32),
             pltpu.VMEM((8, chunk), f32),
             pltpu.VMEM((rank, hidden), f32),
+            pltpu.VMEM((n_dp, cap, chunk), b16),
+            pltpu.VMEM((n_dp, cap, chunk), b16),
+            pltpu.VMEM((n_dp, cap, chunk), b16),
+            pltpu.VMEM((cap, 128), b16),
+            pltpu.VMEM((n_dp, cap, 128), b16),
             dma((6,)), dma((5,)), dma((n_exp,)), dma((n_exp,)), dma((n_exp, 2)), dma((n_exp, 2)),
             dma((2, 3)), dma((2, 3)), dma((n_dp,)), dma((n_dp,)), dma((2, 2)), dma((2, 2)),
+            dma((n_dp,)), dma((n_dp,)), dma((n_dp,)), dma((n_dp,)), dma((n_dp,)), dma((n_dp,)),
         ],
         compiler_params=pltpu.CompilerParams(
             collective_id=0, has_side_effects=True, vmem_limit_bytes=67000000

time: 84.2 us -> 78.8 us (0.936)
  Pallas kernels: 83.4 us -> 78 us
    pallas_call x1, Pallas kernels: 79.3 us -> 73.9 us  [fast(): pl.pallas_call(functools.partial(exchange, n_dp, n_exp, cap, token_mean),...]
where the time goes in v4:
time: 78.8 us; the launch traced here: 78.7 us
  Pallas kernels  78 us (99%)
    pallas_call x1, Pallas kernels, fast(): pl.pallas_call(functools.partial(exchange, n_dp, n_exp, cap, token_mean),...  73.9 us
    pallas_call x1, Pallas kernels, fast(): pl.pallas_call(apply, out_shape=(jax.ShapeDtypeStruct((rows, half), b16),...  4.13 us

profile of v4, /device:TPU:0, one launch (start us, length us, event | category | flops | bytes accessed | tf_op | source)
XLA Modules:
  0.0 78.7 jit_solution(1713241198847839065)
XLA Ops:
  0.6 73.9 %shard_map.85 = (bf16[128,512]{1,0:T(8,128)(2,1)}, f32[64,896]{1,0:T(8,128)}, bf16[896,256]{1,0:T(8,128)(2,1)}, f32[8,896]{1,0:T(8,128)}, f32[64,1024]{1,0:T(8,128)}) custom-call(bf16[128,3584]{1,0:T(8,128)(2,1)} %tok_hbm.1, s32[2,128]{1,0:T(2,128)} %bitcast.11, f32[2,128]{1,0:T(2,128)} %bitcast.12, bf16[3584,1024]{1,0:T(8,128)(2,1)} %bitcast.9, ...), custom_call_target="tpu_custom_call" | custom-call | tf_op jit(solution)/shard_map/pallas_call | solution.py:466
  74.5 4.1 %shard_map.86 = (bf16[128,512]{1,0:T(8,128)(2,1)}, f32[64,896]{1,0:T(8,128)}, f32[896,1024]{1,0:T(8,128)}) custom-call(f32[896,1024]{1,0:T(8,128)} %bitcast.8, bf16[896,256]{1,0:T(8,128)(2,1)} %get-tuple-element.11.left_hbm, f32[8,896]{1,0:T(8,128)} %get-tuple-element.12.recip_hbm, f32[64,1024]{1,0:T(8,128)} %get-tuple-element.13.solved_hbm, ...), custom_call_target="tpu_custom_call" | custom-call | tf_op jit(solution)/shard_map/pallas_call | solution.py:516
